TPU v7x, 32 devices: a whole 2x2x4 slice. The times are simulated.
32 devices in a mesh: band: 8 (over z, y), mem: 4 (over x, core).
Axes of the slice: x: 2, y: 2, z: 4, core: 2. Of those that a mesh axis runs over, the one named last changes fastest.
Arguments:
- ensemble: float32 [128, 5, 32, 128], P('mem', None, 'band'), may hold values from -5 to 5
- obs_value: float32 [256, 128], P(('band', 'mem')), may hold values from -6 to 6
- obs_site: int32 [256, 128], P(('band', 'mem')), may hold values from 0 to 79
- obs_count: int32 [256], P(('band', 'mem')), may hold values from 32 to 128
- obs_precision: float32 [256, 128], P(('band', 'mem')), may hold values from 0.25 to 4
- loc_weight: float32 [256, 3], P(('band', 'mem')), may hold values from 0.1 to 1
- neighbours: int32 [256, 3], P(('band', 'mem')), may hold values from 0 to 7
Outputs:
- forecast: float32 [128, 5, 32, 128], P('mem', None, 'band')
Inputs may be any that keep to these rules, and one draw needn't show every extreme that they name: `obs_site`: site v * 16 + c observes variable v at the tile's c-th cell. Slots 0 to obs_count - 1 of a tile are live. `neighbours`: entries are positions within the aligned block of 8 tiles that holds the tile.
All inputs are finite; a program needn't handle non-finite values.
Results may differ from a plain program's by a relative error of at most 0.0003.
Values sent between devices are 32-bit elements; how exact they have to be, the bound alone decides.
A program may use at most 64 MiB of HBM per device.

v0:
```python
import jax
import jax.numpy as jnp
from jax import lax
from jax.sharding import PartitionSpec as P

TILE = 16
NSI = 6
STEPS = 2
COURANT = 0.08
HIGHEST = lax.Precision.HIGHEST


def extended_2(block, sides, width):
    for axis, dim in sides:
        count = lax.axis_size(axis)
        forward = [(i, i + 1) for i in range(count - 1)]
        backward = [(target, source) for source, target in forward]
        low = lax.ppermute(
            lax.slice_in_dim(block, block.shape[dim] - width, None, axis=dim), axis, forward
        )
        high = lax.ppermute(lax.slice_in_dim(block, 0, width, axis=dim), axis, backward)
        block = jnp.concatenate([low, block, high], axis=dim)
    return block


def minmod(lower_jump, upper_jump):
    return jnp.maximum(0.0, jnp.minimum(lower_jump, upper_jump)) + jnp.minimum(
        0.0, jnp.maximum(lower_jump, upper_jump)
    )


def flux_divergence(halo_extended_field, sweep_direction, advected_field):
    extent = halo_extended_field.shape[sweep_direction]
    differences = lax.slice_in_dim(
        halo_extended_field, 1, extent, axis=sweep_direction
    ) - lax.slice_in_dim(halo_extended_field, 0, extent - 1, axis=sweep_direction)
    slopes = minmod(
        lax.slice_in_dim(differences, 0, extent - 2, axis=sweep_direction),
        lax.slice_in_dim(differences, 1, extent - 1, axis=sweep_direction),
    )
    state_left_side = lax.slice_in_dim(
        halo_extended_field, 1, extent - 2, axis=sweep_direction
    ) + 0.5 * lax.slice_in_dim(slopes, 0, extent - 3, axis=sweep_direction)
    state_right_side = lax.slice_in_dim(
        halo_extended_field, 2, extent - 1, axis=sweep_direction
    ) - 0.5 * lax.slice_in_dim(slopes, 1, extent - 2, axis=sweep_direction)
    advected_field_left = state_left_side[:, advected_field : advected_field + 1]
    advected_field_right = state_right_side[:, advected_field : advected_field + 1]
    signal_velocity = jnp.maximum(jnp.abs(advected_field_left), jnp.abs(advected_field_right))
    interface_fluxes = 0.5 * (
        advected_field_left * state_left_side + advected_field_right * state_right_side
    ) - 0.5 * signal_velocity * (state_right_side - state_left_side)
    return lax.slice_in_dim(
        interface_fluxes, 1, extent - 3, axis=sweep_direction
    ) - lax.slice_in_dim(interface_fluxes, 0, extent - 4, axis=sweep_direction)


def advance(halo_extended_field):
    centre = halo_extended_field[:, :, 2:-2]
    lat_div = flux_divergence(halo_extended_field, 2, 1)
    wrapped = jnp.concatenate([centre[..., -2:], centre, centre[..., :2]], axis=3)
    lon_div = flux_divergence(wrapped, 3, 0)
    return centre - COURANT * (lat_div + lon_div)


def obs_space(tile_state, obs_value, obs_site):
    site_count = tile_state.shape[2]
    ens_mean = jnp.mean(tile_state, axis=1)
    anomaly = tile_state - ens_mean[:, None, :]
    selector = (obs_site[:, :, None] == jnp.arange(site_count)[None, None, :]).astype(jnp.float32)
    obs_anomaly = jnp.einsum("bos,bks->bok", selector, anomaly, precision=HIGHEST)
    obs_mean = jnp.einsum("bos,bs->bo", selector, ens_mean, precision=HIGHEST)
    return (ens_mean, anomaly, obs_anomaly, obs_value - obs_mean)


def transform(local_anomaly, local_innovation, local_weight, ens_mean, anomaly):
    members = local_anomaly.shape[2]
    identity = jnp.eye(members, dtype=jnp.float32)
    weighted = local_anomaly * local_weight[:, :, None]
    gram_matrix = (
        jnp.einsum("bpk,bpj->bkj", weighted, local_anomaly, precision=HIGHEST)
        + (members - 1.0) * identity
    )
    frob_norm = jnp.sqrt(jnp.sum(gram_matrix * gram_matrix, axis=(1, 2)))
    root_iter = gram_matrix / frob_norm[:, None, None]
    inverse = jnp.broadcast_to(identity, gram_matrix.shape)
    for sweep in range(NSI):
        factor = 1.5 * identity - 0.5 * jnp.matmul(inverse, root_iter, precision=HIGHEST)
        root_iter = jnp.matmul(root_iter, factor, precision=HIGHEST)
        inverse = jnp.matmul(factor, inverse, precision=HIGHEST)
    projected = jnp.einsum("bpk,bp->bk", weighted, local_innovation, precision=HIGHEST)
    halfway = jnp.einsum("bkj,bj->bk", inverse, projected, precision=HIGHEST)
    mean_weights = (
        jnp.einsum("bkj,bj->bk", inverse, halfway, precision=HIGHEST) / frob_norm[:, None]
    )
    spread_weights = inverse * jnp.sqrt((members - 1.0) / frob_norm)[:, None, None]
    combined = spread_weights + mean_weights[:, :, None]
    return ens_mean[:, None, :] + jnp.einsum("bjk,bjs->bks", combined, anomaly, precision=HIGHEST)


def localise(obs_anomaly, innovation, slot_weight, neighbour_tiles, loc_weight, ens_mean, anomaly):
    batch_tiles = neighbour_tiles.shape[0]
    local_anomaly = obs_anomaly[neighbour_tiles].reshape(batch_tiles, -1, obs_anomaly.shape[2])
    local_innovation = innovation[neighbour_tiles].reshape(batch_tiles, -1)
    local_weight = (loc_weight[:, :, None] * slot_weight[neighbour_tiles]).reshape(batch_tiles, -1)
    return transform(local_anomaly, local_innovation, local_weight, ens_mean, anomaly)


def shards(ensemble, obs_value, obs_site, obs_count, obs_precision, loc_weight, neighbours):
    fields = ensemble
    lat_rows = fields.shape[2]
    margin = 2 * STEPS
    extended = extended_2(fields, (("band", 2),), margin)
    offset = lax.axis_index("band") * lat_rows
    lat_total = lat_rows * lax.axis_size("band")
    for repeat in range(STEPS):
        extended = advance(extended)
        remaining = margin - 2 * (repeat + 1)
        if remaining > 0:
            global_row = (
                lax.broadcasted_iota(jnp.int32, (1, 1, extended.shape[2], 1), 2)
                - remaining
                + offset
            )
            inside = (global_row >= 0) & (global_row < lat_total)
            extended = jnp.where(inside, extended, 0.0)
    fields = extended
    members, variables, lon_total = (fields.shape[0], fields.shape[1], fields.shape[3])
    flattened = fields.reshape(members, variables, lat_rows * lon_total)
    grouped = lax.all_to_all(flattened, "mem", split_axis=2, concat_axis=0, tiled=True)
    all_members = grouped.shape[0]
    tile_count = neighbours.shape[0]
    tile_state = (
        grouped.reshape(all_members, variables, tile_count, TILE)
        .transpose(2, 0, 1, 3)
        .reshape(tile_count, all_members, variables * TILE)
    )
    ens_mean, anomaly, obs_anomaly, innovation = obs_space(tile_state, obs_value, obs_site)
    live_slots = jnp.arange(obs_value.shape[1])[None, :] < obs_count[:, None]
    slot_weight = jnp.where(live_slots, obs_precision, 0.0)
    analysed = localise(
        obs_anomaly, innovation, slot_weight, neighbours, loc_weight, ens_mean, anomaly
    )
    outgoing = (
        analysed.reshape(tile_count, all_members, variables, TILE)
        .transpose(1, 2, 0, 3)
        .reshape(all_members, variables, tile_count * TILE)
    )
    returned = lax.all_to_all(outgoing, "mem", split_axis=0, concat_axis=2, tiled=True)
    fields = returned.reshape(members, variables, lat_rows, lon_total)
    return advance(extended_2(fields, (("band", 2),), 2))


def solution(mesh):
    return jax.shard_map(
        shards,
        mesh=mesh,
        in_specs=(
            P("mem", None, "band", None),
            P(("band", "mem"), None),
            P(("band", "mem"), None),
            P(("band", "mem")),
            P(("band", "mem"), None),
            P(("band", "mem"), None),
            P(("band", "mem"), None),
        ),
        out_specs=P("mem", None, "band", None),
        check_vma=False,
    )
```

profile of v0, /device:TPU:17, one launch (start us, length us, event | category | flops | bytes accessed | tf_op | source)
XLA Modules:
  0.0 91.0 jit_solution(9798595751797972321)
XLA Ops:
  0.0 1.1 %copy.23 = f32[32,5,4,128]{3,0,2,1:T(8,128)S(1)} copy(f32[32,5,4,128]{3,2,1,0:T(4,128)} %param.7) | data formatting | bytes 655360 | tf_op args[0]
  1.1 3.1 %collective-permute-start = (f32[32,5,4,128]{3,0,2,1:T(8,128)S(1)}, f32[32,5,4,128]{3,0,2,1:T(8,128)S(1)}, u32[]{:S(2)}, u32[]{:S(2)}) collective-permute-start(f32[32,5,4,128]{3,0,2,1:T(8,128)S(1)} %copy.23), channel_id=1, source_target_pairs={{0,4},{4,8},{8,12},{12,16},{16,20},{20,24},{24,28},{1,5},{5,9},{9,... | collective-permute-start | bytes 983048 | tf_op jit(solution)/shard_map/ppermute | solution.py:18
  4.2 3.0 %collective-permute-start.1 = (f32[32,5,4,128]{3,0,2,1:T(8,128)S(1)}, f32[32,5,4,128]{3,0,2,1:T(8,128)S(1)}, u32[]{:S(2)}, u32[]{:S(2)}) collective-permute-start(f32[32,5,4,128]{3,0,2,1:T(8,128)S(1)} %copy.23), channel_id=1, source_target_pairs={{4,0},{8,4},{12,8},{16,12},{20,16},{24,20},{28,24},{5,1},{9,5},{13... | collective-permute-start | bytes 983048 | tf_op jit(solution)/shard_map/ppermute | solution.py:21
  8.1 0.8 fusion.55
  9.5 0.8 copy.33
  10.3 7.3 %collective-permute-done = f32[32,5,4,128]{3,0,2,1:T(8,128)S(1)} collective-permute-done((f32[32,5,4,128]{3,0,2,1:T(8,128)S(1)}, f32[32,5,4,128]{3,0,2,1:T(8,128)S(1)}, u32[]{:S(2)}, u32[]{:S(2)}) %collective-permute-start) | collective-permute-done | bytes 327712 | tf_op jit(solution)/shard_map/ppermute | solution.py:18
  17.7 2.8 %collective-permute-done.1 = f32[32,5,4,128]{3,0,2,1:T(8,128)S(1)} collective-permute-done((f32[32,5,4,128]{3,0,2,1:T(8,128)S(1)}, f32[32,5,4,128]{3,0,2,1:T(8,128)S(1)}, u32[]{:S(2)}, u32[]{:S(2)}) %collective-permute-start.1) | collective-permute-done | bytes 327712 | tf_op jit(solution)/shard_map/ppermute | solution.py:21
  22.4 0.9 fusion.5
  27.7 1.4 %reshape.135 = f32[4,1,20480]{2,1,0:T(1,128)} reshape(f32[512,5,32]{2,1,0:T(8,128)S(1)} %bitcast.129) | data formatting | bytes 655360
  29.1 3.9 %all-to-all-start = ((f32[4,1,20480]{2,1,0:T(1,128)}), f32[4,1,20480]{2,1,0:T(1,128)S(1)}, u32[]{:S(2)}, u32[]{:S(2)}) async-start(f32[4,1,20480]{2,1,0:T(1,128)} %reshape.135), calls=%async_computation | async-start | bytes 655360 | tf_op jit(solution)/shard_map/all_to_all | solution.py:130
  34.3 4.5 %all-to-all-done = f32[4,1,20480]{2,1,0:T(1,128)S(1)} async-done(((f32[4,1,20480]{2,1,0:T(1,128)}), f32[4,1,20480]{2,1,0:T(1,128)S(1)}, u32[]{:S(2)}, u32[]{:S(2)}) %all-to-all-start) | async-done | bytes 327712 | tf_op jit(solution)/shard_map/all_to_all | solution.py:130
  39.2 1.6 %reduce.1 = f32[4,20480]{1,0:T(4,128)S(1)} reduce(f32[4,1,20480]{2,1,0:T(1,128)S(1)} %all-to-all-done, f32[]{:T(128)} %broadcast.188), dimensions={1}, to_apply=%all_to_all.22.reduce_sub_computation | reduce | bytes 655364 | tf_op jit(solution)/shard_map/all_to_all | solution.py:130
  41.5 0.8 copy.55
  45.8 2.8 %multiply_reduce_fusion = (f32[8]{0:T(128)S(1)}, f32[8,128,128]{2,1,0:T(8,128)S(1)}) fusion(f32[128,128]{1,0:T(8,128)} %fusion.52, f32[8,384,128]{2,1,0:T(8,128)S(1)} %bitcast.128, f32[8,384,128]{1,2,0:T(8,128)S(1)} %copy.34, f32[8,384]{1,0:T(8,128)S(1)} %bitcast.135), kind=kOutput, calls=%fused_computation.74 | convolution fusion | flops 604766208 | bytes 3747872 | tf_op jit(solution)/shard_map/bpk,bpj->bkj/dot_general | solution.py:81
  53.8 0.9 fusion.62
  59.5 1.8 %fusion.15 = f32[8,128,1]{1,2,0:T(1,128)S(1)} fusion(f32[8,384,1]{1,2,0:T(1,128)S(1)} %bitcast.137, f32[8,384,128]{1,2,0:T(8,128)S(1)} %copy.34, f32[8,384]{1,0:T(8,128)S(1)} %bitcast.136), kind=kOutput, calls=%fused_computation.32 | convolution fusion | flops 5111808 | bytes 1601536 | tf_op jit(solution)/shard_map/bpk,bp->bk/dot_general | solution.py:91
  62.7 0.9 %convolution_bitcast_fusion = f32[8,128,1]{1,2,0:T(1,128)S(1)} fusion(f32[8,128,128]{2,1,0:T(8,128)S(1)} %fusion.68, f32[8,128,1]{1,2,0:T(1,128)S(1)} %fusion.15), kind=kOutput, calls=%fused_computation.33 | convolution fusion | flops 1572864 | bytes 532480 | tf_op jit(solution)/shard_map/bkj,bj->bk/dot_general | solution.py:92
  63.6 0.9 %fusion.69 = f32[8,1,128]{2,1,0:T(1,128)S(1)} fusion(f32[8,128,128]{2,1,0:T(8,128)S(1)} %fusion.68, f32[8,128,1]{1,2,0:T(1,128)S(1)} %convolution_bitcast_fusion), kind=kOutput, calls=%fused_computation.161 | convolution fusion | flops 1572864 | bytes 532480 | tf_op jit(solution)/shard_map/bkj,bj->bk/dot_general | solution.py:94
  64.6 0.7 convolution_add_fusion
  65.6 11.2 %all_to_all.30 = f32[128,5,128]{2,1,0:T(8,128)S(1)} all-to-all(f32[128,5,128]{2,1,0:T(8,128)S(1)} %copy.36), channel_id=1, replica_groups=mesh['band'=8,'mem'=4] {'mem'}, dimensions={0} | all-to-all | bytes 655360 | tf_op jit(solution)/shard_map/all_to_all | solution.py:149
  77.0 2.3 %collective-permute-start.2 = (f32[32,5,2,128]{3,0,2,1:T(8,128)S(1)}, f32[32,5,2,128]{3,0,2,1:T(8,128)S(1)}, u32[]{:S(2)}, u32[]{:S(2)}) collective-permute-start(f32[32,5,2,128]{3,0,2,1:T(8,128)S(1)} %get-tuple-element.39), channel_id=1, source_target_pairs={{0,4},{4,8},{8,12},{12,16},{16,20},{20,24},{24,28},{1,5},{5,9},{9,... | collective-permute-start | bytes 491528 | tf_op jit(solution)/shard_map/ppermute | solution.py:18
  79.4 3.9 %collective-permute-start.3 = (f32[32,5,2,128]{3,0,2,1:T(8,128)S(1)}, f32[32,5,2,128]{3,0,2,1:T(8,128)S(1)}, u32[]{:S(2)}, u32[]{:S(2)}) collective-permute-start(f32[32,5,2,128]{3,0,2,1:T(8,128)S(1)} %get-tuple-element.40), channel_id=1, source_target_pairs={{4,0},{8,4},{12,8},{16,12},{20,16},{24,20},{28,24},{5,1},{9,5},{13... | collective-permute-start | bytes 491528 | tf_op jit(solution)/shard_map/ppermute | solution.py:21
  84.7 4.7 %collective-permute-done.3 = f32[32,5,2,128]{3,0,2,1:T(8,128)S(1)} collective-permute-done((f32[32,5,2,128]{3,0,2,1:T(8,128)S(1)}, f32[32,5,2,128]{3,0,2,1:T(8,128)S(1)}, u32[]{:S(2)}, u32[]{:S(2)}) %collective-permute-start.3) | collective-permute-done | bytes 163872 | tf_op jit(solution)/shard_map/ppermute | solution.py:21
  90.1 0.9 %copy.38 = f32[32,5,4,128]{3,2,1,0:T(4,128)} copy(f32[32,5,4,128]{3,0,2,1:T(8,128)S(1)} %fusion.38) | data formatting | bytes 655360 | tf_op jit(solution)/shard_map/sub | solution.py:63
  (112 shorter events, 27.3 us)
Async XLA Ops:
  0.0 17.7 %copy-start = (f32[32,5,4,128]{3,2,1,0:T(4,128)S(1)}, f32[32,5,4,128]{3,2,1,0:T(4,128)}, u32[]{:S(2)}) copy-start(f32[32,5,4,128]{3,2,1,0:T(4,128)} %param.7) | copy-start | bytes 983044
  1.1 16.6 %collective-permute-start = (f32[32,5,4,128]{3,0,2,1:T(8,128)S(1)}, f32[32,5,4,128]{3,0,2,1:T(8,128)S(1)}, u32[]{:S(2)}, u32[]{:S(2)}) collective-permute-start(f32[32,5,4,128]{3,0,2,1:T(8,128)S(1)} %copy.23), channel_id=1, source_target_pairs={{0,4},{4,8},{8,12},{12,16},{16,20},{20,24},{24,28},{1,5},{5,9},{9,... | collective-permute-start | bytes 983048 | tf_op jit(solution)/shard_map/ppermute | solution.py:18
  4.2 16.3 %collective-permute-start.1 = (f32[32,5,4,128]{3,0,2,1:T(8,128)S(1)}, f32[32,5,4,128]{3,0,2,1:T(8,128)S(1)}, u32[]{:S(2)}, u32[]{:S(2)}) collective-permute-start(f32[32,5,4,128]{3,0,2,1:T(8,128)S(1)} %copy.23), channel_id=1, source_target_pairs={{4,0},{8,4},{12,8},{16,12},{20,16},{24,20},{28,24},{5,1},{9,5},{13... | collective-permute-start | bytes 983048 | tf_op jit(solution)/shard_map/ppermute | solution.py:21
  29.1 9.7 %all-to-all-start = ((f32[4,1,20480]{2,1,0:T(1,128)}), f32[4,1,20480]{2,1,0:T(1,128)S(1)}, u32[]{:S(2)}, u32[]{:S(2)}) async-start(f32[4,1,20480]{2,1,0:T(1,128)} %reshape.135), calls=%async_computation | async-start | bytes 655360 | tf_op jit(solution)/shard_map/all_to_all | solution.py:130
  42.9 1.1 %copy-start.4 = (s32[8,128]{1,0:T(8,128)S(1)}, s32[8,128]{1,0:T(8,128)}, u32[]{:S(2)}) copy-start(s32[8,128]{1,0:T(8,128)} %param.9) | copy-start | bytes 12292
  43.2 0.7 copy-start.2
  45.8 2.8 %copy-start.1 = (f32[128,128]{1,0:T(8,128)S(1)}, f32[128,128]{1,0:T(8,128)}, u32[]{:S(2)}) copy-start(f32[128,128]{1,0:T(8,128)} %fusion.53) | copy-start | bytes 196612
  57.3 1.3 %copy-start.5 = (s32[8,128]{1,0:T(8,128)S(1)}, s32[8,128]{1,0:T(8,128)}, u32[]{:S(2)}) copy-start(s32[8,128]{1,0:T(8,128)} %param.9) | copy-start | bytes 12292
  57.3 1.3 %copy-start.7 = (f32[8,80,1]{1,0,2:T(8,128)S(1)}, f32[8,80,1]{1,0,2:T(8,128)}, u32[]{:S(2)}) copy-start(f32[8,80,1]{1,0,2:T(8,128)} %reshape.125) | copy-start | bytes 7684
  57.3 1.6 %copy-start.6 = (f32[8,128]{1,0:T(8,128)S(1)}, f32[8,128]{1,0:T(8,128)}, u32[]{:S(2)}) copy-start(f32[8,128]{1,0:T(8,128)} %param.8) | copy-start | bytes 12292
  62.0 2.6 %copy-start.3 = (f32[8,80]{1,0:T(8,128)S(1)}, f32[8,80]{1,0:T(8,128)}, u32[]{:S(2)}) copy-start(f32[8,80]{1,0:T(8,128)} %copy-done.2) | copy-start | bytes 7684
  77.0 7.7 %collective-permute-start.2 = (f32[32,5,2,128]{3,0,2,1:T(8,128)S(1)}, f32[32,5,2,128]{3,0,2,1:T(8,128)S(1)}, u32[]{:S(2)}, u32[]{:S(2)}) collective-permute-start(f32[32,5,2,128]{3,0,2,1:T(8,128)S(1)} %get-tuple-element.39), channel_id=1, source_target_pairs={{0,4},{4,8},{8,12},{12,16},{16,20},{20,24},{24,28},{1,5},{5,9},{9,... | collective-permute-start | bytes 491528 | tf_op jit(solution)/shard_map/ppermute | solution.py:18
  79.4 10.1 %collective-permute-start.3 = (f32[32,5,2,128]{3,0,2,1:T(8,128)S(1)}, f32[32,5,2,128]{3,0,2,1:T(8,128)S(1)}, u32[]{:S(2)}, u32[]{:S(2)}) collective-permute-start(f32[32,5,2,128]{3,0,2,1:T(8,128)S(1)} %get-tuple-element.40), channel_id=1, source_target_pairs={{4,0},{8,4},{12,8},{16,12},{20,16},{24,20},{28,24},{5,1},{9,5},{13... | collective-permute-start | bytes 491528 | tf_op jit(solution)/shard_map/ppermute | solution.py:21
where the time goes:
time: 91.5 us; the launch traced here: 91 us
  waiting for transfers between devices  19.3 us (21%)
  matrix products  19.3 us (21%)
  starting transfers between devices  16.3 us (18%)
  other arithmetic  12.6 us (14%)
  local copies, waits for them, and re-layouts  11.7 us (13%)
  blocking collectives  11.2 us (12%)
    all_to_all x1, blocking collectives, shards(): lax.all_to_all(outgoing, 'mem', split_axis=0, concat_axis=2, tiled=True)  11.2 us
    ppermute x2, waiting for transfers between devices, extended_2(): lax.ppermute(lax.slice_in_dim(block, 0, width, axis=dim), axis, backward)  7.53 us
    ppermute x2, waiting for transfers between devices, extended_2(): lax.ppermute(lax.slice_in_dim(block, block.shape[dim] - width, None, axis...  7.3 us
    ppermute x2, starting transfers between devices, extended_2(): lax.ppermute(lax.slice_in_dim(block, 0, width, axis=dim), axis, backward)  6.89 us
    ppermute x2, starting transfers between devices, extended_2(): lax.ppermute(lax.slice_in_dim(block, block.shape[dim] - width, None, axis...  5.48 us
    all_to_all x1, waiting for transfers between devices, shards(): lax.all_to_all(flattened, 'mem', split_axis=2, concat_axis=0, tiled=True)  4.47 us
    dot_general x6, matrix products, transform(): inverse = jnp.matmul(factor, inverse, precision=HIGHEST)  4.05 us
    unnamed x23, local copies, waits for them, and re-layouts  3.95 us
  transfers between devices with their start and end apart: 5, of which 4 were waited for; matrix products, arithmetic and copies ran while one was open for 6% of the time, Pallas kernels for 0%

commit v1 on v0

--- a/solution.py
+++ b/solution.py
@@ -127,7 +127,10 @@
     fields = extended
     members, variables, lon_total = (fields.shape[0], fields.shape[1], fields.shape[3])
     flattened = fields.reshape(members, variables, lat_rows * lon_total)
-    grouped = lax.all_to_all(flattened, "mem", split_axis=2, concat_axis=0, tiled=True)
+    grouped = jnp.concatenate(
+        lax.all_to_all(jnp.stack(jnp.split(flattened, lax.axis_size("mem"), axis=2)), "mem", 0, 0),
+        axis=0,
+    )
     all_members = grouped.shape[0]
     tile_count = neighbours.shape[0]
     tile_state = (

time: 91.5 us -> 87.1 us (0.952)
  local copies, waits for them, and re-layouts: 11.7 us -> 8.14 us
    unnamed x23 -> x21, local copies, waits for them, and re-layouts: 3.95 us -> 1.92 us
    all_to_all x1 -> x0, other arithmetic: 1.56 us -> none  [shards(): lax.all_to_all(flattened, 'mem', split_axis=2, concat_axis=0, tiled=True)]
    reshape x2 -> x0, local copies, waits for them, and re-layouts: 1.25 us -> none  [the longest x1 0.69 us: shards(): flattened = fields.reshape(members, variables, lat_rows * lon_total)]
  transfers between devices with their start and end apart: 5 -> 5, of which waited for: 4 -> 4; matrix products, arithmetic and copies ran while one was open for 6% -> 7% of each run, Pallas kernels for 0% -> 0%
where the time goes in v1:
time: 87.1 us; the launch traced here: 86.6 us
  waiting for transfers between devices  19.3 us (22%)
  matrix products  19.3 us (22%)
  starting transfers between devices  16.3 us (19%)
  other arithmetic  11.8 us (14%)
  blocking collectives  11.1 us (13%)
  local copies, waits for them, and re-layouts  8.14 us (9%)
    all_to_all x1, blocking collectives, shards(): lax.all_to_all(outgoing, 'mem', split_axis=0, concat_axis=2, tiled=True)  11.1 us
    ppermute x2, waiting for transfers between devices, extended_2(): lax.ppermute(lax.slice_in_dim(block, 0, width, axis=dim), axis, backward)  7.53 us
    ppermute x2, waiting for transfers between devices, extended_2(): lax.ppermute(lax.slice_in_dim(block, block.shape[dim] - width, None, axis...  7.3 us
    ppermute x2, starting transfers between devices, extended_2(): lax.ppermute(lax.slice_in_dim(block, 0, width, axis=dim), axis, backward)  6.88 us
    ppermute x2, starting transfers between devices, extended_2(): lax.ppermute(lax.slice_in_dim(block, block.shape[dim] - width, None, axis...  5.48 us
    all_to_all x1, waiting for transfers between devices, shards(): lax.all_to_all(jnp.stack(jnp.split(flattened, lax.axis_size('mem'), axis=...  4.47 us
    dot_general x6, matrix products, transform(): inverse = jnp.matmul(factor, inverse, precision=HIGHEST)  4.03 us
    all_to_all x1, starting transfers between devices, shards(): lax.all_to_all(jnp.stack(jnp.split(flattened, lax.axis_size('mem'), axis=...  3.92 us
  transfers between devices with their start and end apart: 5, of which 4 were waited for; matrix products, arithmetic and copies ran while one was open for 7% of the time, Pallas kernels for 0%

profile of v1, /device:TPU:17, one launch (start us, length us, event | category | flops | bytes accessed | tf_op | source)
XLA Modules:
  0.0 86.6 jit_solution(12158899793693394315)
XLA Ops:
  0.0 1.1 %copy.23 = f32[32,5,4,128]{3,0,2,1:T(8,128)S(1)} copy(f32[32,5,4,128]{3,2,1,0:T(4,128)} %param.7) | data formatting | bytes 655360 | tf_op args[0]
  1.1 3.1 %collective-permute-start = (f32[32,5,4,128]{3,0,2,1:T(8,128)S(1)}, f32[32,5,4,128]{3,0,2,1:T(8,128)S(1)}, u32[]{:S(2)}, u32[]{:S(2)}) collective-permute-start(f32[32,5,4,128]{3,0,2,1:T(8,128)S(1)} %copy.23), channel_id=1, source_target_pairs={{0,4},{4,8},{8,12},{12,16},{16,20},{20,24},{24,28},{1,5},{5,9},{9,... | collective-permute-start | bytes 983048 | tf_op jit(solution)/shard_map/ppermute | solution.py:18
  4.2 3.0 %collective-permute-start.1 = (f32[32,5,4,128]{3,0,2,1:T(8,128)S(1)}, f32[32,5,4,128]{3,0,2,1:T(8,128)S(1)}, u32[]{:S(2)}, u32[]{:S(2)}) collective-permute-start(f32[32,5,4,128]{3,0,2,1:T(8,128)S(1)} %copy.23), channel_id=1, source_target_pairs={{4,0},{8,4},{12,8},{16,12},{20,16},{24,20},{28,24},{5,1},{9,5},{13... | collective-permute-start | bytes 983048 | tf_op jit(solution)/shard_map/ppermute | solution.py:21
  7.3 0.7 compare_select_fusion
  8.1 0.8 fusion.56
  9.5 0.8 copy.31
  10.3 7.3 %collective-permute-done = f32[32,5,4,128]{3,0,2,1:T(8,128)S(1)} collective-permute-done((f32[32,5,4,128]{3,0,2,1:T(8,128)S(1)}, f32[32,5,4,128]{3,0,2,1:T(8,128)S(1)}, u32[]{:S(2)}, u32[]{:S(2)}) %collective-permute-start) | collective-permute-done | bytes 327712 | tf_op jit(solution)/shard_map/ppermute | solution.py:18
  17.7 2.8 %collective-permute-done.1 = f32[32,5,4,128]{3,0,2,1:T(8,128)S(1)} collective-permute-done((f32[32,5,4,128]{3,0,2,1:T(8,128)S(1)}, f32[32,5,4,128]{3,0,2,1:T(8,128)S(1)}, u32[]{:S(2)}, u32[]{:S(2)}) %collective-permute-start.1) | collective-permute-done | bytes 327712 | tf_op jit(solution)/shard_map/ppermute | solution.py:21
  22.4 0.9 %fusion.5 = (f32[32,5,8,129]{3,0,2,1:T(8,128)S(1)}, f32[32,5,8,129]{3,0,2,1:T(8,128)S(1)}) fusion(f32[32,5,8,130]{3,0,2,1:T(8,128)S(1)} %minimum_add_fusion, f32[32,5,8,128]{3,0,2,1:T(8,128)S(1)} %slice.346, f32[32,5,8,2]{3,0,2,1:T(8,128)S(1)} %get-tuple-element.18, f32[32,5,8,2]{3,0,2,1:T(8,128)S(1)} %get-tuple-element.19), kind=kLoop, calls=%fused_computation.11 | loop fusion | flops 990720 | bytes 3317760 | tf_op jit(solution)/shard_map/add | solution.py:41
  27.0 0.8 pad_maximum_fusion.12
  27.8 3.9 %all-to-all-start = ((f32[4,32,5,128]{3,1,2,0:T(8,128)}), f32[4,32,5,128]{3,1,2,0:T(8,128)S(1)}, u32[]{:S(2)}, u32[]{:S(2)}) async-start(f32[4,32,5,128]{3,1,2,0:T(8,128)} %pad_maximum_fusion.12), calls=%async_computation | async-start | bytes 655360 | tf_op jit(solution)/shard_map/all_to_all | solution.py:131
  33.0 4.5 %all-to-all-done = f32[4,32,5,128]{3,1,2,0:T(8,128)S(1)} async-done(((f32[4,32,5,128]{3,1,2,0:T(8,128)}), f32[4,32,5,128]{3,1,2,0:T(8,128)S(1)}, u32[]{:S(2)}, u32[]{:S(2)}) %all-to-all-start) | async-done | bytes 327712 | tf_op jit(solution)/shard_map/all_to_all | solution.py:131
  41.4 2.8 %multiply_reduce_fusion = (f32[8]{0:T(128)S(1)}, f32[8,128,128]{2,1,0:T(8,128)S(1)}) fusion(f32[128,128]{1,0:T(8,128)} %fusion.53, f32[8,384,128]{2,1,0:T(8,128)S(1)} %bitcast.133, f32[8,384,128]{1,2,0:T(8,128)S(1)} %copy.32, f32[8,384]{1,0:T(8,128)S(1)} %bitcast.137), kind=kOutput, calls=%fused_computation.73 | convolution fusion | flops 604766208 | bytes 3747872 | tf_op jit(solution)/shard_map/bpk,bpj->bkj/dot_general | solution.py:81
  44.8 0.7 fusion.52
  51.4 0.9 fusion.65
  55.1 1.8 %fusion.15 = f32[8,128,1]{1,2,0:T(1,128)S(1)} fusion(f32[8,384,1]{1,2,0:T(1,128)S(1)} %bitcast.139, f32[8,384,128]{1,2,0:T(8,128)S(1)} %copy.32, f32[8,384]{1,0:T(8,128)S(1)} %bitcast.138), kind=kOutput, calls=%fused_computation.31 | convolution fusion | flops 5111808 | bytes 1601536 | tf_op jit(solution)/shard_map/bpk,bp->bk/dot_general | solution.py:91
  58.3 0.9 %convolution_bitcast_fusion = f32[8,128,1]{1,2,0:T(1,128)S(1)} fusion(f32[8,128,128]{2,1,0:T(8,128)S(1)} %fusion.69, f32[8,128,1]{1,2,0:T(1,128)S(1)} %fusion.15), kind=kOutput, calls=%fused_computation.32 | convolution fusion | flops 1572864 | bytes 532480 | tf_op jit(solution)/shard_map/bkj,bj->bk/dot_general | solution.py:92
  59.2 0.9 %fusion.70 = f32[8,1,128]{2,1,0:T(1,128)S(1)} fusion(f32[8,128,128]{2,1,0:T(8,128)S(1)} %fusion.69, f32[8,128,1]{1,2,0:T(1,128)S(1)} %convolution_bitcast_fusion), kind=kOutput, calls=%fused_computation.167 | convolution fusion | flops 1572864 | bytes 532480 | tf_op jit(solution)/shard_map/bkj,bj->bk/dot_general | solution.py:94
  60.2 0.7 convolution_add_fusion
  61.2 11.1 %all_to_all.20 = f32[128,5,128]{2,1,0:T(8,128)S(1)} all-to-all(f32[128,5,128]{2,1,0:T(8,128)S(1)} %copy.34), channel_id=1, replica_groups=mesh['band'=8,'mem'=4] {'mem'}, dimensions={0} | all-to-all | bytes 655360 | tf_op jit(solution)/shard_map/all_to_all | solution.py:152
  72.6 2.3 %collective-permute-start.2 = (f32[32,5,2,128]{3,0,2,1:T(8,128)S(1)}, f32[32,5,2,128]{3,0,2,1:T(8,128)S(1)}, u32[]{:S(2)}, u32[]{:S(2)}) collective-permute-start(f32[32,5,2,128]{3,0,2,1:T(8,128)S(1)} %get-tuple-element.39), channel_id=1, source_target_pairs={{0,4},{4,8},{8,12},{12,16},{16,20},{20,24},{24,28},{1,5},{5,9},{9,... | collective-permute-start | bytes 491528 | tf_op jit(solution)/shard_map/ppermute | solution.py:18
  75.0 3.9 %collective-permute-start.3 = (f32[32,5,2,128]{3,0,2,1:T(8,128)S(1)}, f32[32,5,2,128]{3,0,2,1:T(8,128)S(1)}, u32[]{:S(2)}, u32[]{:S(2)}) collective-permute-start(f32[32,5,2,128]{3,0,2,1:T(8,128)S(1)} %get-tuple-element.40), channel_id=1, source_target_pairs={{4,0},{8,4},{12,8},{16,12},{20,16},{24,20},{28,24},{5,1},{9,5},{13... | collective-permute-start | bytes 491528 | tf_op jit(solution)/shard_map/ppermute | solution.py:21
  80.3 4.7 %collective-permute-done.3 = f32[32,5,2,128]{3,0,2,1:T(8,128)S(1)} collective-permute-done((f32[32,5,2,128]{3,0,2,1:T(8,128)S(1)}, f32[32,5,2,128]{3,0,2,1:T(8,128)S(1)}, u32[]{:S(2)}, u32[]{:S(2)}) %collective-permute-start.3) | collective-permute-done | bytes 163872 | tf_op jit(solution)/shard_map/ppermute | solution.py:21
  85.7 0.9 %copy.36 = f32[32,5,4,128]{3,2,1,0:T(4,128)} copy(f32[32,5,4,128]{3,0,2,1:T(8,128)S(1)} %fusion.38) | data formatting | bytes 655360 | tf_op jit(solution)/shard_map/sub | solution.py:63
  (109 shorter events, 24.6 us)
Async XLA Ops:
  0.0 17.7 %copy-start = (f32[32,5,4,128]{3,2,1,0:T(4,128)S(1)}, f32[32,5,4,128]{3,2,1,0:T(4,128)}, u32[]{:S(2)}) copy-start(f32[32,5,4,128]{3,2,1,0:T(4,128)} %param.7) | copy-start | bytes 983044
  1.1 16.6 %collective-permute-start = (f32[32,5,4,128]{3,0,2,1:T(8,128)S(1)}, f32[32,5,4,128]{3,0,2,1:T(8,128)S(1)}, u32[]{:S(2)}, u32[]{:S(2)}) collective-permute-start(f32[32,5,4,128]{3,0,2,1:T(8,128)S(1)} %copy.23), channel_id=1, source_target_pairs={{0,4},{4,8},{8,12},{12,16},{16,20},{20,24},{24,28},{1,5},{5,9},{9,... | collective-permute-start | bytes 983048 | tf_op jit(solution)/shard_map/ppermute | solution.py:18
  4.2 16.3 %collective-permute-start.1 = (f32[32,5,4,128]{3,0,2,1:T(8,128)S(1)}, f32[32,5,4,128]{3,0,2,1:T(8,128)S(1)}, u32[]{:S(2)}, u32[]{:S(2)}) collective-permute-start(f32[32,5,4,128]{3,0,2,1:T(8,128)S(1)} %copy.23), channel_id=1, source_target_pairs={{4,0},{8,4},{12,8},{16,12},{20,16},{24,20},{28,24},{5,1},{9,5},{13... | collective-permute-start | bytes 983048 | tf_op jit(solution)/shard_map/ppermute | solution.py:21
  27.8 9.7 %all-to-all-start = ((f32[4,32,5,128]{3,1,2,0:T(8,128)}), f32[4,32,5,128]{3,1,2,0:T(8,128)S(1)}, u32[]{:S(2)}, u32[]{:S(2)}) async-start(f32[4,32,5,128]{3,1,2,0:T(8,128)} %pad_maximum_fusion.12), calls=%async_computation | async-start | bytes 655360 | tf_op jit(solution)/shard_map/all_to_all | solution.py:131
  38.5 1.1 %copy-start.4 = (s32[8,128]{1,0:T(8,128)S(1)}, s32[8,128]{1,0:T(8,128)}, u32[]{:S(2)}) copy-start(s32[8,128]{1,0:T(8,128)} %param.9) | copy-start | bytes 12292
  38.8 0.7 copy-start.2
  41.4 2.8 %copy-start.1 = (f32[128,128]{1,0:T(8,128)S(1)}, f32[128,128]{1,0:T(8,128)}, u32[]{:S(2)}) copy-start(f32[128,128]{1,0:T(8,128)} %fusion.54) | copy-start | bytes 196612
  52.9 1.3 %copy-start.5 = (s32[8,128]{1,0:T(8,128)S(1)}, s32[8,128]{1,0:T(8,128)}, u32[]{:S(2)}) copy-start(s32[8,128]{1,0:T(8,128)} %param.9) | copy-start | bytes 12292
  52.9 1.3 %copy-start.7 = (f32[8,80,1]{1,0,2:T(8,128)S(1)}, f32[8,80,1]{1,0,2:T(8,128)}, u32[]{:S(2)}) copy-start(f32[8,80,1]{1,0,2:T(8,128)} %reshape.120) | copy-start | bytes 7684
  52.9 1.6 %copy-start.6 = (f32[8,128]{1,0:T(8,128)S(1)}, f32[8,128]{1,0:T(8,128)}, u32[]{:S(2)}) copy-start(f32[8,128]{1,0:T(8,128)} %param.8) | copy-start | bytes 12292
  57.6 2.6 %copy-start.3 = (f32[8,80]{1,0:T(8,128)S(1)}, f32[8,80]{1,0:T(8,128)}, u32[]{:S(2)}) copy-start(f32[8,80]{1,0:T(8,128)} %copy-done.2) | copy-start | bytes 7684
  72.6 7.7 %collective-permute-start.2 = (f32[32,5,2,128]{3,0,2,1:T(8,128)S(1)}, f32[32,5,2,128]{3,0,2,1:T(8,128)S(1)}, u32[]{:S(2)}, u32[]{:S(2)}) collective-permute-start(f32[32,5,2,128]{3,0,2,1:T(8,128)S(1)} %get-tuple-element.39), channel_id=1, source_target_pairs={{0,4},{4,8},{8,12},{12,16},{16,20},{20,24},{24,28},{1,5},{5,9},{9,... | collective-permute-start | bytes 491528 | tf_op jit(solution)/shard_map/ppermute | solution.py:18
  75.0 10.1 %collective-permute-start.3 = (f32[32,5,2,128]{3,0,2,1:T(8,128)S(1)}, f32[32,5,2,128]{3,0,2,1:T(8,128)S(1)}, u32[]{:S(2)}, u32[]{:S(2)}) collective-permute-start(f32[32,5,2,128]{3,0,2,1:T(8,128)S(1)} %get-tuple-element.40), channel_id=1, source_target_pairs={{4,0},{8,4},{12,8},{16,12},{20,16},{24,20},{28,24},{5,1},{9,5},{13... | collective-permute-start | bytes 491528 | tf_op jit(solution)/shard_map/ppermute | solution.py:21
